TPU v7x, 256 devices: a whole 4x4x8 slice. The times are simulated.
256 devices in a mesh: cell: 32 (over y_hi, z, core), brick: 8 (over x, y_lo).
Axes of the slice: x: 4, y: 4 (y_hi: 2, y_lo: 2; y = y_hi * 2 + y_lo), z: 8, core: 2. Of those that a mesh axis runs over, the one named last changes fastest.
Arguments:
- features: bfloat16 [32, 8, 128, 256], P('cell', 'brick'), may hold values from -6 to 6
- species: int32 [32, 8, 128], P('cell', 'brick'), may hold values from 0 to 3
- species_table: bfloat16 [4, 256], replicated, may hold values from -3 to 3
- neighbours: int32 [32, 8, 64, 128], P('cell', 'brick'), may hold values from 0 to 383
- counts: int32 [32, 8, 128], P('cell', 'brick'), may hold values from 1 to 64
- send_lists: int32 [32, 8, 8, 32], P('cell', 'brick'), may hold values from 0 to 127
- distances: float32 [32, 8, 64, 128], P('cell', 'brick'), may hold values from 0.05 to 1
- head_decay: float32 [8], replicated, may hold values from 0.25 to 4
- norm_gain: float32 [256], replicated, may hold values from 0.5 to 1.5
- readout: float32 [256], replicated, may hold values from -0.375 to 0.375
- targets: float32 [32, 8, 128], P('cell', 'brick'), may hold values from -6 to 6
- master: float32 [4, 256, 256], P(None, 'cell'), as said below
- moment: float32 [4, 256, 256], P(None, 'cell'), may hold values from -3 to 3
- second: float32 [4, 256, 256], P(None, 'cell'), may hold values from 0.1 to 1
Outputs:
- energies: float32 [32, 8, 128], P('cell', 'brick')
- moment_new: float32 [4, 256, 256], P(None, 'cell')
- second_new: float32 [4, 256, 256], P(None, 'cell')
- adam_step: float32 [4, 256, 256], P(None, 'cell')
Inputs may be any that keep to these rules, and one draw needn't show every extreme that they name: `master`: projection entries lie within -48 * 256^-0.5 and 48 * 256^-0.5.
All inputs are finite; a program needn't handle non-finite values.
Results may differ from a plain program's by a relative error of at most 0.0045.
The roundings to bfloat16 on the way count: a program that leaves them out, or rounds other values in their place, can miss the bound.
Values may be sent and summed in bfloat16 or wider, within the bound.
A program may use at most 64 MiB of HBM per device.

v0:
```python
import math
import jax
import jax.numpy as jnp
from jax import lax
from jax.sharding import PartitionSpec as P

TILE = 128
loss_weight = 0.0625
epsilon_norm = 1e-06


def silu_slope(inputs):
    sigmoid_val = jax.nn.sigmoid(inputs)
    return sigmoid_val * (1.0 + inputs * (1.0 - sigmoid_val))


def normalize(embedded, norm_gain):
    rms_scale = lax.rsqrt(jnp.mean(embedded * embedded, axis=-1, keepdims=True) + epsilon_norm)
    return (embedded * rms_scale * norm_gain).astype(jnp.bfloat16)


def brick_sweep(
    query,
    key_table,
    value_table,
    embedded,
    neighbour_rows,
    local_count,
    local_dist,
    local_target,
    out_proj,
    head_decay,
    readout,
):
    atom_count, model_width = query.shape
    head_count = head_decay.shape[0]
    head_size = model_width // head_count
    slot_count = neighbour_rows.shape[0]
    score_scale = 1.0 / math.sqrt(head_size)
    table_rows = key_table.shape[0]

    def tile_step(grad_carry, tile_index):
        key_grads, value_grads = grad_carry
        key_rows = key_table[neighbour_rows].reshape(slot_count, TILE, head_count, head_size)
        value_rows = value_table[neighbour_rows].reshape(slot_count, TILE, head_count, head_size)
        query_heads = query.reshape(TILE, head_count, head_size)
        is_valid = (jnp.arange(slot_count)[:, None] < local_count[None, :])[:, :, None]
        score = (
            jnp.einsum("ahd,kahd->kah", query_heads, key_rows, preferred_element_type=jnp.float32)
            * score_scale
        )
        score = score - head_decay[None, None, :] * local_dist[:, :, None]
        score = jnp.where(is_valid, score, -1e30)
        row_max = jnp.max(score, axis=0, keepdims=True)
        exp_terms = jnp.where(is_valid, jnp.exp(score - row_max), 0.0)
        attention = exp_terms / jnp.sum(exp_terms, axis=0, keepdims=True)
        attention_half = attention.astype(jnp.bfloat16)
        attended = jnp.einsum(
            "kah,kahd->ahd", attention_half, value_rows, preferred_element_type=jnp.float32
        )
        attended = attended.astype(jnp.bfloat16).reshape(TILE, model_width)
        updated = embedded + jnp.dot(attended, out_proj, preferred_element_type=jnp.float32)
        energy = jnp.sum(readout * jax.nn.silu(updated), axis=-1)
        grad_energy = loss_weight * (energy - local_target)
        grad_updated = (grad_energy[:, None] * readout * silu_slope(updated)).astype(jnp.bfloat16)
        grad_attended = jnp.einsum(
            "ad,cd->ac", grad_updated, out_proj, preferred_element_type=jnp.float32
        ).astype(jnp.bfloat16)
        grad_att_heads = grad_attended.reshape(TILE, head_count, head_size)
        grad_weights = jnp.einsum(
            "ahd,kahd->kah", grad_att_heads, value_rows, preferred_element_type=jnp.float32
        )
        grad_score = attention * (
            grad_weights - jnp.sum(attention * grad_weights, axis=0, keepdims=True)
        )
        grad_score = grad_score.astype(jnp.bfloat16)
        grad_query = (
            jnp.einsum("kah,kahd->ahd", grad_score, key_rows, preferred_element_type=jnp.float32)
            * score_scale
        )
        grad_query = grad_query.astype(jnp.bfloat16).reshape(TILE, model_width)
        key_edge = (
            grad_score.astype(jnp.float32)[..., None]
            * query_heads.astype(jnp.float32)[None]
            * score_scale
        )
        value_edge = (
            attention_half.astype(jnp.float32)[..., None] * grad_att_heads.astype(jnp.float32)[None]
        )
        flattened_rows = neighbour_rows.reshape(-1)
        key_grads = key_grads.at[flattened_rows].add(key_edge.reshape(-1, model_width))
        value_grads = value_grads.at[flattened_rows].add(value_edge.reshape(-1, model_width))
        return ((key_grads, value_grads), (energy, attended, grad_updated, grad_query))

    start_grads = (
        jnp.zeros((table_rows, model_width), jnp.float32),
        jnp.zeros((table_rows, model_width), jnp.float32),
    )
    (key_grads, value_grads), stacked = lax.scan(
        tile_step, start_grads, jnp.arange(atom_count // TILE, dtype=jnp.int32)
    )
    energy, attended, grad_updated, grad_query = stacked
    return (
        key_grads,
        value_grads,
        energy.reshape(atom_count),
        attended.reshape(atom_count, model_width),
        grad_updated.reshape(atom_count, model_width),
        grad_query.reshape(atom_count, model_width),
    )


def body(
    features,
    species,
    species_table,
    neighbours,
    counts,
    send_lists,
    distances,
    head_decay,
    norm_gain,
    readout,
    targets,
    master,
    moment,
    second,
):
    local_feat = features[0, 0]
    local_species = species[0, 0]
    neighbour_rows = neighbours[0, 0]
    local_count = counts[0, 0]
    send_rows = send_lists[0, 0]
    local_dist = distances[0, 0]
    local_target = targets[0, 0]
    atom_count, model_width = local_feat.shape
    bricks, ghost_position = send_rows.shape
    species_count = species_table.shape[0]
    picked = (local_species[:, None] == jnp.arange(species_count)[None, :]).astype(jnp.bfloat16)
    embedded = local_feat.astype(jnp.float32) + jnp.dot(
        picked, species_table, preferred_element_type=jnp.float32
    )
    normed_features = normalize(embedded, norm_gain)
    attention_weights = lax.all_gather(master.astype(jnp.bfloat16), "cell", axis=1, tiled=True)
    projected = jnp.einsum(
        "pe,mer->mpr", normed_features, attention_weights[0:3], preferred_element_type=jnp.float32
    ).astype(jnp.bfloat16)
    flat_send = send_rows.reshape(-1)
    parcel = projected[1:3][:, flat_send].reshape(2, bricks, ghost_position, model_width)
    arrived = lax.all_to_all(parcel, "brick", split_axis=1, concat_axis=1, tiled=True)
    ghost_keys = arrived[0].reshape(-1, model_width)
    ghost_values = arrived[1].reshape(-1, model_width)
    key_table = jnp.concatenate([projected[1], ghost_keys], axis=0)
    value_table = jnp.concatenate([projected[2], ghost_values], axis=0)
    key_grads, value_grads, energy, attended, grad_updated, grad_query = brick_sweep(
        projected[0],
        key_table,
        value_table,
        embedded,
        neighbour_rows,
        local_count,
        local_dist,
        local_target,
        attention_weights[3],
        head_decay,
        readout,
    )
    ghost_grads = jnp.stack([key_grads[atom_count:], value_grads[atom_count:]]).reshape(
        2, bricks, ghost_position, model_width
    )
    returned = lax.all_to_all(
        ghost_grads.astype(jnp.bfloat16), "brick", split_axis=1, concat_axis=1, tiled=True
    ).astype(ghost_grads.dtype)
    local_portion = jnp.stack([key_grads[:atom_count], value_grads[:atom_count]])
    totals = (
        local_portion.at[:, flat_send]
        .add(returned.reshape(2, -1, model_width))
        .astype(jnp.bfloat16)
    )
    grad_q = jnp.einsum(
        "ac,ad->cd", normed_features, grad_query, preferred_element_type=jnp.float32
    )
    key_gradient = jnp.einsum(
        "ac,ad->cd", normed_features, totals[0], preferred_element_type=jnp.float32
    )
    grad_v = jnp.einsum("ac,ad->cd", normed_features, totals[1], preferred_element_type=jnp.float32)
    grad_o = jnp.einsum("ac,ad->cd", attended, grad_updated, preferred_element_type=jnp.float32)
    grads = jnp.stack([grad_q, key_gradient, grad_v, grad_o])
    summed = lax.psum(grads.astype(jnp.bfloat16), "brick")
    owned = lax.psum_scatter(summed, "cell", scatter_dimension=1, tiled=True).astype(jnp.float32)
    moment_new = 0.9 * moment + 0.1 * owned
    second_new = 0.999 * second + 0.001 * owned * owned
    adam_step = moment_new / (jnp.sqrt(second_new) + 1e-08)
    return (energy[None, None, :], moment_new, second_new, adam_step)


def solution(mesh):
    return jax.shard_map(
        body,
        mesh=mesh,
        in_specs=(
            P("cell", "brick", None, None),
            P("cell", "brick", None),
            P(),
            P("cell", "brick", None, None),
            P("cell", "brick", None),
            P("cell", "brick", None, None),
            P("cell", "brick", None, None),
            P(),
            P(),
            P(),
            P("cell", "brick", None),
            P(None, "cell", None),
            P(None, "cell", None),
            P(None, "cell", None),
        ),
        out_specs=(
            P("cell", "brick", None),
            P(None, "cell", None),
            P(None, "cell", None),
            P(None, "cell", None),
        ),
        check_vma=False,
    )
```

profile of v0, /device:TPU:16, one launch (start us, length us, event | category | flops | bytes accessed | tf_op | source)
XLA Modules:
  0.0 491.4 jit_solution(7539827670805211175)
XLA Ops:
  7.2 0.0 copy-start
  7.2 0.8 reshape_squeeze.17
  8.0 0.8 convert_element_type.79
  8.7 1.2 multiply_reduce_fusion.5
  9.9 43.4 %all_gather.3 = bf16[4,256,256]{2,1,0:T(8,128)(2,1)S(1)} all-gather(bf16[4,8,256]{2,1,0:T(8,128)(2,1)S(1)} %convert_element_type.79), channel_id=1, replica_groups=mesh['cell'=32,'brick'=8] {'cell'}, dimensions={1}, use_global_device_ids=true | all-gather | bytes 540672 | tf_op jit(solution)/shard_map/all_gather | solution.py:144
  53.3 0.8 multiply_convert_fusion.2
  54.1 0.2 fusion.10
  54.3 0.1 copy.52
  54.5 1.2 gather_fusion
  55.7 0.7 copy.53
  56.4 5.9 %all-to-all-start = ((bf16[2,8,32,256]{3,2,0,1:T(8,128)(2,1)}), bf16[2,8,32,256]{3,2,0,1:T(8,128)(2,1)S(1)}, u32[]{:S(2)}, u32[]{:S(2)}) async-start(bf16[2,8,32,256]{3,2,0,1:T(8,128)(2,1)} %copy.53), calls=%async_computation | async-start | bytes 524288 | tf_op jit(solution)/shard_map/all_to_all | solution.py:150
  62.4 0.8 compare_select_fusion
  63.2 0.7 iota_compare_fusion.2
  63.8 0.1 copy.56
  64.0 0.8 fusion.37
  64.8 5.0 %all-to-all-done = bf16[2,8,32,256]{3,2,0,1:T(8,128)(2,1)S(1)} async-done(((bf16[2,8,32,256]{3,2,0,1:T(8,128)(2,1)}), bf16[2,8,32,256]{3,2,0,1:T(8,128)(2,1)S(1)}, u32[]{:S(2)}, u32[]{:S(2)}) %all-to-all-start) | async-done | bytes 262176 | tf_op jit(solution)/shard_map/all_to_all | solution.py:150
  69.9 32.9 %gather_fusion.1 = bf16[8192,256]{1,0:T(8,128)(2,1)} fusion(bf16[384,256]{1,0:T(8,128)(2,1)S(1)} %get-tuple-element.81, s32[8192]{0:T(1024)S(1)} %fusion.37), kind=kCustom, calls=%fused_computation.1 | custom fusion | bytes 8421376 | tf_op jit(solution)/shard_map/while/body/eval_jaxpr/gather | solution.py:44
  102.8 6.4 %copy.55 = bf16[8192,256]{0,1:T(8,128)(2,1)} copy(bf16[8192,256]{1,0:T(8,128)(2,1)} %gather_fusion.1) | data formatting | bytes 8388608 | tf_op jit(solution)/shard_map/while/body/eval_jaxpr/gather | solution.py:44
  109.2 5.3 %copy.103 = bf16[32,8,64,128]{3,2,1,0:T(8,128)(2,1)} copy(bf16[32,8,64,128]{3,1,2,0:T(8,128)(2,1)} %bitcast.154) | data formatting | bytes 8388608
  114.5 32.9 %gather_fusion.2 = bf16[8192,256]{1,0:T(8,128)(2,1)} fusion(bf16[384,256]{1,0:T(8,128)(2,1)S(1)} %get-tuple-element.82, s32[8192]{0:T(1024)S(1)} %fusion.37), kind=kCustom, calls=%fused_computation.2 | custom fusion | bytes 8421376 | tf_op jit(solution)/shard_map/while/body/eval_jaxpr/gather | solution.py:45
  147.4 6.7 %copy.58 = bf16[8192,256]{0,1:T(8,128)(2,1)} copy(bf16[8192,256]{1,0:T(8,128)(2,1)} %gather_fusion.2) | data formatting | bytes 8388608 | tf_op jit(solution)/shard_map/while/body/eval_jaxpr/gather | solution.py:45
  154.2 0.0 copy-start.7
  154.2 5.5 %copy.104 = bf16[32,8,64,128]{3,2,1,0:T(8,128)(2,1)} copy(bf16[32,8,64,128]{3,1,2,0:T(8,128)(2,1)} %bitcast.155) | data formatting | bytes 8388608
  159.7 1.2 multiply_reduce_fusion.3
  160.9 1.1 convert_convert_fusion
  162.0 4.0 multiply_reduce_fusion.2
  166.0 0.3 multiply_reduce_fusion.4
  166.3 0.0 copy-start.8
  166.3 0.2 convolution_convert_fusion.5
  166.6 0.1 copy.59
  166.7 3.4 multiply_reduce_fusion.1
  170.1 1.1 broadcast_multiply_fusion
  171.2 22.6 %copy.118 = f32[32,8,64,128]{3,1,2,0:T(8,128)} copy(f32[32,8,64,128]{3,2,1,0:T(8,128)S(1)} %bitcast.150) | data formatting | bytes 16777216
  193.8 9.0 %copy.61 = f32[8192,256]{1,0:T(8,128)} copy(f32[8192,256]{0,1:T(8,128)} %bitcast.152) | data formatting | bytes 16777216 | tf_op jit(solution)/shard_map/while/body/eval_jaxpr/mul | solution.py:88
  202.8 44.7 %scatter_custom_fusion.1 = f32[384,256]{1,0:T(8,128)S(1)} fusion(s32[8192]{0:T(1024)S(1)} %bitcast.169, f32[8192,256]{1,0:T(8,128)} %copy.61, f32[]{:T(128)} %constant.16.clone.1), kind=kCustom, calls=%fused_computation.51 | custom fusion | flops 2097152 | bytes 393728 | tf_op jit(solution)/shard_map/while/body/eval_jaxpr/scatter-add | solution.py:92
  247.6 0.2 bitcast_convert_fusion
  247.8 1.2 multiply_multiply_fusion
  249.1 10.9 %copy.119 = f32[32,8,64,128]{3,1,2,0:T(8,128)} copy(f32[32,8,64,128]{3,2,1,0:T(8,128)S(1)} %bitcast.151) | data formatting | bytes 16777216
  259.9 9.0 %copy.60 = f32[8192,256]{1,0:T(8,128)} copy(f32[8192,256]{0,1:T(8,128)} %bitcast.153) | data formatting | bytes 16777216 | tf_op jit(solution)/shard_map/while/body/eval_jaxpr/mul | solution.py:83
  268.9 44.9 %scatter_custom_fusion = f32[384,256]{1,0:T(8,128)S(1)} fusion(s32[8192]{0:T(1024)S(1)} %bitcast.170, f32[8192,256]{1,0:T(8,128)} %copy.60, f32[]{:T(128)} %constant.16.clone.1), kind=kCustom, calls=%fused_computation.53 | custom fusion | flops 2097152 | bytes 393728 | tf_op jit(solution)/shard_map/while/body/eval_jaxpr/scatter-add | solution.py:91
  313.9 0.0 copy-start.1
  313.9 4.0 multiply_reduce_fusion
  318.0 0.2 copy.65
  318.2 0.7 pad_maximum_fusion.2
  318.9 3.4 all-to-all-start.1
  322.3 0.0 reduce-scatter.4.cloned.1.call-start
  322.4 0.2 fusion.11
  322.6 0.2 fusion.14
  322.8 6.4 %all-to-all-done.1 = bf16[2,8,32,256]{3,2,0,1:T(8,128)(2,1)S(1)} async-done(((bf16[2,8,32,256]{3,2,0,1:T(8,128)(2,1)}), bf16[2,8,32,256]{3,2,0,1:T(8,128)(2,1)S(1)}, u32[]{:S(2)}, u32[]{:S(2)}) %all-to-all-start.1) | async-done | bytes 262176 | tf_op jit(solution)/shard_map/all_to_all | solution.py:171
  329.2 0.1 convert_bitcast_fusion
  329.3 0.4 copy.66
  329.7 8.9 %scatter_fusion = f32[2,128,256]{2,0,1:T(2,128)S(1)} fusion(f32[2,128,256]{2,0,1:T(2,128)S(1)} %copy.65, s32[256]{0:T(256)S(1)} %bitcast.172, f32[256,2,256]{2,1,0:T(2,128)S(1)} %copy.66), kind=kCustom, calls=%fused_computation.5 | custom fusion | flops 131072 | bytes 1573888 | tf_op jit(solution)/shard_map/scatter-add | solution.py:177
  338.6 0.1 convert_element_type.92
  338.7 0.2 fusion.53
  338.9 0.2 fusion.12
  339.1 0.2 fusion.13
  339.3 0.1 pad_maximum_fusion
  339.4 0.4 copy.93
  339.8 0.9 copy.107
  340.7 0.0 reduce-scatter.4.cloned.1.call-update
  340.7 108.5 %reduce-scatter.4.cloned.1.call-done = bf16[8,1024]{1,0:T(8,128)(2,1)} async-done(((bf16[256,1024]{1,0:T(8,128)(2,1)}), bf16[8,1024]{1,0:T(8,128)(2,1)}) %reduce-scatter.4.cloned.1.call-update) | async-done | bytes 16400
  449.1 0.7 reshape.281
  449.9 33.8 %psum.8 = bf16[4,8,256]{2,1,0:T(8,128)(2,1)S(1)} all-reduce(bf16[4,8,256]{2,1,0:T(8,128)(2,1)S(1)} %copy.94), channel_id=1, replica_groups=mesh['cell'=32,'brick'=8] {'brick'}, use_global_device_ids=true, to_apply=%region_8.9 | all-reduce | flops 8192 | bytes 32768 | tf_op jit(solution)/shard_map/psum | solution.py:189
  483.7 0.6 add_divide_fusion.1
  (32 shorter events, 0.3 us)
Async XLA Ops:
  7.2 1.6 copy-start
  56.4 13.4 %all-to-all-start = ((bf16[2,8,32,256]{3,2,0,1:T(8,128)(2,1)}), bf16[2,8,32,256]{3,2,0,1:T(8,128)(2,1)S(1)}, u32[]{:S(2)}, u32[]{:S(2)}) async-start(bf16[2,8,32,256]{3,2,0,1:T(8,128)(2,1)} %copy.53), calls=%async_computation | async-start | bytes 524288 | tf_op jit(solution)/shard_map/all_to_all | solution.py:150
  154.1 5.6 %copy-start.2 = (bf16[32,8,64,128]{3,2,1,0:T(8,128)(2,1)S(1)}, bf16[32,8,64,128]{3,2,1,0:T(8,128)(2,1)}, u32[]{:S(2)}) copy-start(bf16[32,8,64,128]{3,2,1,0:T(8,128)(2,1)} %copy.103) | copy-start | bytes 12582916
  154.2 6.7 %copy-start.6 = (f32[8]{0:T(128)S(1)}, f32[8]{0:T(128)}, u32[]{:S(2)}) copy-start(f32[8]{0:T(128)} %param.21) | copy-start | bytes 100
  154.2 11.8 %copy-start.5 = (f32[256]{0:T(256)S(1)}, f32[256]{0:T(256)}, u32[]{:S(2)}) copy-start(f32[256]{0:T(256)} %param.23) | copy-start | bytes 3076
  154.2 12.1 %copy-start.7 = (f32[1,1,128]{2,1,0:T(1,128)S(1)}, f32[1,1,128]{2,1,0:T(1,128)}, u32[]{:S(2)}) copy-start(f32[1,1,128]{2,1,0:T(1,128)} %param.24) | copy-start | bytes 1540
  166.3 27.5 %copy-start.8 = (f32[128]{0:T(128)}, f32[128]{0:T(128)S(1)}, u32[]{:S(2)}) copy-start(f32[128]{0:T(128)S(1)} %get-tuple-element.78) | copy-start | bytes 1540
  313.9 170.5 %copy-start.1 = (bf16[4,256]{1,0:T(4,128)(2,1)S(1)}, bf16[4,256]{1,0:T(4,128)(2,1)}, u32[]{:S(2)}) copy-start(bf16[4,256]{1,0:T(4,128)(2,1)} %param.16) | copy-start | bytes 6148
  313.9 169.8 %copy-start.3 = (f32[4,8,256]{2,1,0:T(8,128)S(1)}, f32[4,8,256]{2,1,0:T(8,128)}, u32[]{:S(2)}) copy-start(f32[4,8,256]{2,1,0:T(8,128)} %param.27) | copy-start | bytes 98308
  313.9 169.8 %copy-start.4 = (f32[4,8,256]{2,1,0:T(8,128)S(1)}, f32[4,8,256]{2,1,0:T(8,128)}, u32[]{:S(2)}) copy-start(f32[4,8,256]{2,1,0:T(8,128)} %param.26) | copy-start | bytes 98308
  318.9 10.3 %all-to-all-start.1 = ((bf16[2,8,32,256]{3,2,0,1:T(8,128)(2,1)}), bf16[2,8,32,256]{3,2,0,1:T(8,128)(2,1)S(1)}, u32[]{:S(2)}, u32[]{:S(2)}) async-start(bf16[2,8,32,256]{3,2,0,1:T(8,128)(2,1)} %pad_maximum_fusion.2), calls=%async_computation.1 | async-start | bytes 524288 | tf_op jit(solution)/shard_map/all_to_all | solution.py:171
  322.3 126.8 %reduce-scatter.4.cloned.1.call-start = ((), (), s32[]{:S(2)}) async-start(), calls=%async_computation.3 | async-start | bytes 540672
Sparse Core Ops, SparseCore 0:
  340.8 108.2 reduce-scatter.3
where the time goes:
time: 496 us; the launch traced here: 491 us
  local copies, waits for them, and re-layouts  147 us (30%)
  other arithmetic  120 us (24%)
  waiting for transfers between devices  120 us (24%)
  blocking collectives  77.2 us (16%)
  between operations  14.7 us (3%)
  starting transfers between devices  9.37 us (2%)
    unnamed x2, waiting for transfers between devices  108 us
    unnamed x26, local copies, waits for them, and re-layouts  46.4 us
    scatter-add x1, other arithmetic, tile_step(): key_grads.at[flattened_rows].add(key_edge.reshape(-1, model_width))  44.9 us
    scatter-add x1, other arithmetic, tile_step(): value_grads.at[flattened_rows].add(value_edge.reshape(-1, model_width))  44.7 us
    all_gather x1, blocking collectives, body(): lax.all_gather(master.astype(jnp.bfloat16), 'cell', axis=1, tiled=True)  43.4 us
    gather x2, local copies, waits for them, and re-layouts, tile_step(): value_table[neighbour_rows].reshape(slot_count, TILE, head_count, head_size)  39.7 us
    gather x2, local copies, waits for them, and re-layouts, tile_step(): key_table[neighbour_rows].reshape(slot_count, TILE, head_count, head_size)  39.3 us
    psum x1, blocking collectives, body(): summed = lax.psum(grads.astype(jnp.bfloat16), 'brick')  33.8 us
  transfers between devices with their start and end apart: 3, of which 3 were waited for; matrix products, arithmetic and copies ran while one was open for 1% of the time, Pallas kernels for 0%

commit v1 on v0

--- a/solution.py
+++ b/solution.py
@@ -186,7 +186,7 @@
     grad_v = jnp.einsum("ac,ad->cd", normed_features, totals[1], preferred_element_type=jnp.float32)
     grad_o = jnp.einsum("ac,ad->cd", attended, grad_updated, preferred_element_type=jnp.float32)
     grads = jnp.stack([grad_q, key_gradient, grad_v, grad_o])
-    summed = lax.psum(grads.astype(jnp.bfloat16), "brick")
+    summed = jnp.sum(lax.all_gather(grads.astype(jnp.bfloat16), "brick"), axis=0)
     owned = lax.psum_scatter(summed, "cell", scatter_dimension=1, tiled=True).astype(jnp.float32)
     moment_new = 0.9 * moment + 0.1 * owned
     second_new = 0.999 * second + 0.001 * owned * owned

time: 496 us -> 561 us (1.13)
  waiting for transfers between devices: 120 us -> 213 us
  blocking collectives: 77.2 us -> 43.4 us
    all_gather x0 -> x1, waiting for transfers between devices: none -> 86.7 us  [body(): lax.all_gather(grads.astype(jnp.bfloat16), 'brick')]
    psum x1 -> x0, blocking collectives: 33.8 us -> none  [body(): summed = lax.psum(grads.astype(jnp.bfloat16), 'brick')]
    unnamed x2 -> x3, waiting for transfers between devices: 108 us -> 115 us
    unnamed x26 -> x25, local copies, waits for them, and re-layouts: 46.4 us -> 46.4 us
  transfers between devices with their start and end apart: 3 -> 4, of which waited for: 3 -> 4; matrix products, arithmetic and copies ran while one was open for 1% -> 1% of each run, Pallas kernels for 0% -> 0%
where the time goes in v1:
time: 561 us; the launch traced here: 555 us
  waiting for transfers between devices  213 us (38%)
  local copies, waits for them, and re-layouts  147 us (26%)
  other arithmetic  124 us (22%)
  blocking collectives  43.4 us (8%)
  between operations  14.7 us (3%)
  starting transfers between devices  9.41 us (2%)
    unnamed x3, waiting for transfers between devices  115 us
    all_gather x1, waiting for transfers between devices, body(): lax.all_gather(grads.astype(jnp.bfloat16), 'brick')  86.7 us
    unnamed x25, local copies, waits for them, and re-layouts  46.4 us
    scatter-add x1, other arithmetic, tile_step(): key_grads.at[flattened_rows].add(key_edge.reshape(-1, model_width))  44.9 us
    scatter-add x1, other arithmetic, tile_step(): value_grads.at[flattened_rows].add(value_edge.reshape(-1, model_width))  44.7 us
    all_gather x1, blocking collectives, body(): lax.all_gather(master.astype(jnp.bfloat16), 'cell', axis=1, tiled=True)  43.4 us
    gather x2, local copies, waits for them, and re-layouts, tile_step(): value_table[neighbour_rows].reshape(slot_count, TILE, head_count, head_size)  39.7 us
    gather x2, local copies, waits for them, and re-layouts, tile_step(): key_table[neighbour_rows].reshape(slot_count, TILE, head_count, head_size)  39.3 us
  transfers between devices with their start and end apart: 4, of which 4 were waited for; matrix products, arithmetic and copies ran while one was open for 1% of the time, Pallas kernels for 0%

profile of v1, /device:TPU:16, one launch (start us, length us, event | category | flops | bytes accessed | tf_op | source)
XLA Modules:
  0.0 554.5 jit_solution(18028913034369532969)
XLA Ops:
  7.2 0.0 copy-start
  7.2 0.8 reshape_squeeze.17
  8.0 0.8 convert_element_type.88
  8.7 1.2 multiply_reduce_fusion.5
  9.9 43.4 %all_gather.7 = bf16[4,256,256]{2,1,0:T(8,128)(2,1)S(1)} all-gather(bf16[4,8,256]{2,1,0:T(8,128)(2,1)S(1)} %convert_element_type.88), channel_id=1, replica_groups=mesh['cell'=32,'brick'=8] {'cell'}, dimensions={1}, use_global_device_ids=true | all-gather | bytes 540672 | tf_op jit(solution)/shard_map/all_gather | solution.py:144
  53.3 0.8 multiply_convert_fusion.2
  54.1 0.2 fusion.10
  54.3 0.1 copy.52
  54.5 1.2 gather_fusion
  55.7 0.7 copy.53
  56.4 5.9 %all-to-all-start = ((bf16[2,8,32,256]{3,2,0,1:T(8,128)(2,1)}), bf16[2,8,32,256]{3,2,0,1:T(8,128)(2,1)S(1)}, u32[]{:S(2)}, u32[]{:S(2)}) async-start(bf16[2,8,32,256]{3,2,0,1:T(8,128)(2,1)} %copy.53), calls=%async_computation | async-start | bytes 524288 | tf_op jit(solution)/shard_map/all_to_all | solution.py:150
  62.4 0.8 compare_select_fusion
  63.2 0.7 iota_compare_fusion.2
  63.8 0.1 copy.56
  64.0 0.8 fusion.37
  64.8 5.0 all-to-all-done
  69.9 32.9 %gather_fusion.1 = bf16[8192,256]{1,0:T(8,128)(2,1)} fusion(bf16[384,256]{1,0:T(8,128)(2,1)S(1)} %get-tuple-element.81, s32[8192]{0:T(1024)S(1)} %fusion.37), kind=kCustom, calls=%fused_computation.1 | custom fusion | bytes 8421376 | tf_op jit(solution)/shard_map/while/body/eval_jaxpr/gather | solution.py:44
  102.8 6.4 %copy.55 = bf16[8192,256]{0,1:T(8,128)(2,1)} copy(bf16[8192,256]{1,0:T(8,128)(2,1)} %gather_fusion.1) | data formatting | bytes 8388608 | tf_op jit(solution)/shard_map/while/body/eval_jaxpr/gather | solution.py:44
  109.2 5.3 copy.103
  114.5 32.9 %gather_fusion.2 = bf16[8192,256]{1,0:T(8,128)(2,1)} fusion(bf16[384,256]{1,0:T(8,128)(2,1)S(1)} %get-tuple-element.82, s32[8192]{0:T(1024)S(1)} %fusion.37), kind=kCustom, calls=%fused_computation.2 | custom fusion | bytes 8421376 | tf_op jit(solution)/shard_map/while/body/eval_jaxpr/gather | solution.py:45
  147.4 6.7 %copy.58 = bf16[8192,256]{0,1:T(8,128)(2,1)} copy(bf16[8192,256]{1,0:T(8,128)(2,1)} %gather_fusion.2) | data formatting | bytes 8388608 | tf_op jit(solution)/shard_map/while/body/eval_jaxpr/gather | solution.py:45
  154.2 5.5 copy.104
  159.7 1.2 multiply_reduce_fusion.3
  160.9 1.1 convert_convert_fusion
  162.0 4.0 multiply_reduce_fusion.2
  166.0 0.3 multiply_reduce_fusion.4
  166.3 0.2 convolution_convert_fusion.5
  166.6 0.1 copy.59
  166.7 3.4 multiply_reduce_fusion.1
  170.1 1.1 broadcast_multiply_fusion
  171.2 22.6 %copy.122 = f32[32,8,64,128]{3,1,2,0:T(8,128)} copy(f32[32,8,64,128]{3,2,1,0:T(8,128)S(1)} %bitcast.150) | data formatting | bytes 16777216
  193.8 9.0 %copy.61 = f32[8192,256]{1,0:T(8,128)} copy(f32[8192,256]{0,1:T(8,128)} %bitcast.152) | data formatting | bytes 16777216 | tf_op jit(solution)/shard_map/while/body/eval_jaxpr/mul | solution.py:88
  202.8 44.7 %scatter_custom_fusion.1 = f32[384,256]{1,0:T(8,128)S(1)} fusion(s32[8192]{0:T(1024)S(1)} %bitcast.169, f32[8192,256]{1,0:T(8,128)} %copy.61, f32[]{:T(128)} %constant.17.clone.1), kind=kCustom, calls=%fused_computation.51 | custom fusion | flops 2097152 | bytes 393728 | tf_op jit(solution)/shard_map/while/body/eval_jaxpr/scatter-add | solution.py:92
  247.6 0.2 bitcast_convert_fusion
  247.8 1.2 multiply_multiply_fusion
  249.1 10.9 %copy.123 = f32[32,8,64,128]{3,1,2,0:T(8,128)} copy(f32[32,8,64,128]{3,2,1,0:T(8,128)S(1)} %bitcast.151) | data formatting | bytes 16777216
  259.9 9.0 %copy.60 = f32[8192,256]{1,0:T(8,128)} copy(f32[8192,256]{0,1:T(8,128)} %bitcast.153) | data formatting | bytes 16777216 | tf_op jit(solution)/shard_map/while/body/eval_jaxpr/mul | solution.py:83
  268.9 44.9 %scatter_custom_fusion = f32[384,256]{1,0:T(8,128)S(1)} fusion(s32[8192]{0:T(1024)S(1)} %bitcast.170, f32[8192,256]{1,0:T(8,128)} %copy.60, f32[]{:T(128)} %constant.17.clone.1), kind=kCustom, calls=%fused_computation.53 | custom fusion | flops 2097152 | bytes 393728 | tf_op jit(solution)/shard_map/while/body/eval_jaxpr/scatter-add | solution.py:91
  313.9 4.0 multiply_reduce_fusion
  318.0 0.2 copy.65
  318.2 0.7 pad_maximum_fusion.2
  318.9 3.4 all-to-all-start.1
  322.3 0.0 all-gather.2.cloned.1.call-start
  322.4 0.2 fusion.11
  322.6 0.2 fusion.14
  322.8 6.4 %all-to-all-done.1 = bf16[2,8,32,256]{3,2,0,1:T(8,128)(2,1)S(1)} async-done(((bf16[2,8,32,256]{3,2,0,1:T(8,128)(2,1)}), bf16[2,8,32,256]{3,2,0,1:T(8,128)(2,1)S(1)}, u32[]{:S(2)}, u32[]{:S(2)}) %all-to-all-start.1) | async-done | bytes 262176 | tf_op jit(solution)/shard_map/all_to_all | solution.py:171
  329.2 0.1 convert_bitcast_fusion
  329.3 0.4 copy.66
  329.7 8.9 %scatter_fusion = f32[2,128,256]{2,0,1:T(2,128)S(1)} fusion(f32[2,128,256]{2,0,1:T(2,128)S(1)} %copy.65, s32[256]{0:T(256)S(1)} %bitcast.172, f32[256,2,256]{2,1,0:T(2,128)S(1)} %copy.66), kind=kCustom, calls=%fused_computation.5 | custom fusion | flops 131072 | bytes 1573888 | tf_op jit(solution)/shard_map/scatter-add | solution.py:177
  338.6 0.1 convert_element_type.101
  338.7 0.2 fusion.53
  338.9 0.2 fusion.12
  339.1 0.2 fusion.13
  339.3 0.9 pad_maximum_fusion
  340.1 0.0 all-gather.2.cloned.1.call-update
  340.2 0.0 reduce-scatter.4.cloned.1.call-start
  340.2 86.7 %all-gather.2.cloned.1.call-done = bf16[8,4,256,256]{3,2,1,0:T(8,128)(2,1)} async-done(((bf16[1,4,256,256]{3,2,1,0:T(8,128)(2,1)}), bf16[8,4,256,256]{3,2,1,0:T(8,128)(2,1)}) %all-gather.2.cloned.1.call-update) | async-done | bytes 4194320 | tf_op jit(solution)/shard_map/all_gather | solution.py:189
  426.9 2.8 reduce_sum.55
  429.8 0.4 copy.93
  430.2 0.9 copy.107
  431.1 0.0 reduce-scatter.4.cloned.1.call-update
  431.1 115.0 %reduce-scatter.4.cloned.1.call-done = bf16[8,1024]{1,0:T(8,128)(2,1)} async-done(((bf16[256,1024]{1,0:T(8,128)(2,1)}), bf16[8,1024]{1,0:T(8,128)(2,1)}) %reduce-scatter.4.cloned.1.call-update) | async-done | bytes 16400
  546.1 0.7 reshape.344
  546.8 0.6 add_divide_fusion.1
  (34 shorter events, 0.3 us)
Async XLA Ops:
  7.2 1.6 copy-start
  56.4 13.4 %all-to-all-start = ((bf16[2,8,32,256]{3,2,0,1:T(8,128)(2,1)}), bf16[2,8,32,256]{3,2,0,1:T(8,128)(2,1)S(1)}, u32[]{:S(2)}, u32[]{:S(2)}) async-start(bf16[2,8,32,256]{3,2,0,1:T(8,128)(2,1)} %copy.53), calls=%async_computation | async-start | bytes 524288 | tf_op jit(solution)/shard_map/all_to_all | solution.py:150
  154.1 5.6 %copy-start.2 = (bf16[32,8,64,128]{3,2,1,0:T(8,128)(2,1)S(1)}, bf16[32,8,64,128]{3,2,1,0:T(8,128)(2,1)}, u32[]{:S(2)}) copy-start(bf16[32,8,64,128]{3,2,1,0:T(8,128)(2,1)} %copy.103) | copy-start | bytes 12582916
  154.2 6.7 %copy-start.6 = (f32[8]{0:T(128)S(1)}, f32[8]{0:T(128)}, u32[]{:S(2)}) copy-start(f32[8]{0:T(128)} %param.21) | copy-start | bytes 100
  154.2 11.8 %copy-start.5 = (f32[256]{0:T(256)S(1)}, f32[256]{0:T(256)}, u32[]{:S(2)}) copy-start(f32[256]{0:T(256)} %param.23) | copy-start | bytes 3076
  154.2 12.1 %copy-start.7 = (f32[1,1,128]{2,1,0:T(1,128)S(1)}, f32[1,1,128]{2,1,0:T(1,128)}, u32[]{:S(2)}) copy-start(f32[1,1,128]{2,1,0:T(1,128)} %param.24) | copy-start | bytes 1540
  166.3 27.5 %copy-start.8 = (f32[128]{0:T(128)}, f32[128]{0:T(128)S(1)}, u32[]{:S(2)}) copy-start(f32[128]{0:T(128)S(1)} %get-tuple-element.78) | copy-start | bytes 1540
  317.9 228.9 %copy-start.3 = (f32[4,8,256]{2,1,0:T(8,128)S(1)}, f32[4,8,256]{2,1,0:T(8,128)}, u32[]{:S(2)}) copy-start(f32[4,8,256]{2,1,0:T(8,128)} %param.27) | copy-start | bytes 98308
  317.9 228.9 %copy-start.4 = (f32[4,8,256]{2,1,0:T(8,128)S(1)}, f32[4,8,256]{2,1,0:T(8,128)}, u32[]{:S(2)}) copy-start(f32[4,8,256]{2,1,0:T(8,128)} %param.26) | copy-start | bytes 98308
  317.9 229.5 %copy-start.1 = (bf16[4,256]{1,0:T(4,128)(2,1)S(1)}, bf16[4,256]{1,0:T(4,128)(2,1)}, u32[]{:S(2)}) copy-start(bf16[4,256]{1,0:T(4,128)(2,1)} %param.16) | copy-start | bytes 6148
  318.9 10.3 %all-to-all-start.1 = ((bf16[2,8,32,256]{3,2,0,1:T(8,128)(2,1)}), bf16[2,8,32,256]{3,2,0,1:T(8,128)(2,1)S(1)}, u32[]{:S(2)}, u32[]{:S(2)}) async-start(bf16[2,8,32,256]{3,2,0,1:T(8,128)(2,1)} %pad_maximum_fusion.2), calls=%async_computation.1 | async-start | bytes 524288 | tf_op jit(solution)/shard_map/all_to_all | solution.py:171
  322.3 104.6 %all-gather.2.cloned.1.call-start = ((), (), s32[]{:S(2)}) async-start(), calls=%async_computation.3 | async-start | bytes 4718592 | tf_op jit(solution)/shard_map/all_gather | solution.py:189
  340.2 205.9 %reduce-scatter.4.cloned.1.call-start = ((), (), s32[]{:S(2)}) async-start(), calls=%async_computation.4 | async-start | bytes 540672
Sparse Core Ops, SparseCore 0:
  340.3 86.5 all-gather.1
  431.2 114.8 reduce-scatter.3
